TPU v7x, 512 devices: a whole 4x8x8 slice. The times are simulated.
512 devices in a mesh: src: 128 (over y, z, core), depth: 4 (over x).
Axes of the slice: x: 4, y: 8, z: 8, core: 2. Of those that a mesh axis runs over, the one named last changes fastest.
Arguments:
- incident: float32 [128, 4, 2, 4096], P('src'), may hold values from -6 to 6
- encode: int32 [128], P('src'), may hold values from 0 to 15
- freq_index: int32 [128], P('src'), may hold values from 0 to 7
- wavenum: float32 [8], replicated, may hold values from 1 to 2.8
- slowness: float32 [4, 4096], P('depth'), may hold values from -6 to 6
- probes: bfloat16 [64, 4, 4096], P(None, 'depth'), may hold values from -6 to 6
Outputs:
- sketch_basis: float32 [64, 4, 4096], P(None, 'depth', 'src')
- r_factor: float32 [64, 64], replicated
All inputs are finite; a program needn't handle non-finite values.
Results may differ from a plain program's by a relative error of at most 0.02.
Values may be sent and summed in bfloat16 or wider, within the bound.
A program may use at most 128 MiB of HBM per device.

v0:
```python
import math
import jax
import jax.numpy as jnp
from jax import lax
from jax.sharding import PartitionSpec as P

SIDE = 64
DAMPING = 0.5
STEP_DEPTH = 1.0


def from_behind(x, axis, by):
    size = lax.axis_size(axis)
    pairs = [(i, i + by) for i in range(size) if 0 <= i + by < size]
    return lax.ppermute(x, axis, pairs)


def dft_tables(points, direction):
    counter = jnp.arange(points, dtype=jnp.int32)
    product = counter[:, None] * counter[None, :] % points
    angles = 2.0 * math.pi / points * product.astype(jnp.float32)
    cosine = jnp.cos(angles) / math.sqrt(points)
    sine_part = direction * jnp.sin(angles) / math.sqrt(points)
    matrix = jnp.stack(
        [jnp.stack([cosine, sine_part], axis=1), jnp.stack([-sine_part, cosine], axis=1)], axis=0
    )
    matrix = matrix.astype(jnp.bfloat16)
    total_points = points * points
    twist_index = counter[:, None] * counter[None, :] % total_points
    twist_angle = 2.0 * math.pi / total_points * twist_index.astype(jnp.float32)
    return (matrix, jnp.cos(twist_angle), direction * jnp.sin(twist_angle))


def transform(values, tables):
    matrix, twist_real, twist_imag = tables
    points = matrix.shape[1]
    leading = values.shape[:-2]
    grid_values = values.reshape((-1, 2 * points, points))
    square = matrix.reshape(2 * points, 2 * points)
    segmented = jnp.einsum("nkb,km->nbm", grid_values, square, preferred_element_type=jnp.float32)
    real_part = segmented[:, :, :points]
    imag_part = segmented[:, :, points:]
    turned = jnp.concatenate(
        [
            real_part * twist_real - imag_part * twist_imag,
            real_part * twist_imag + imag_part * twist_real,
        ],
        axis=-1,
    )
    turned = turned.astype(jnp.bfloat16).reshape((-1, points, 2, points))
    result = jnp.einsum("nbsc,sbtd->ntdc", turned, matrix, preferred_element_type=jnp.float32)
    return result.reshape(leading + (2, points * points))


def complex_times(first, second):
    real_part = first[..., 0, :] * second[..., 0, :] - first[..., 1, :] * second[..., 1, :]
    imag_part = first[..., 0, :] * second[..., 1, :] + first[..., 1, :] * second[..., 0, :]
    return jnp.stack([real_part, imag_part], axis=-2)


def conjugate(values):
    return jnp.stack([values[..., 0, :], -values[..., 1, :]], axis=-2)


def propagate(values, spectrum, forward, inverse):
    moved_on = transform(values.astype(jnp.bfloat16), forward)
    return transform(complex_times(moved_on, spectrum).astype(jnp.bfloat16), inverse)


def propagator(wave_nums, points_all):
    counter = jnp.arange(points_all, dtype=jnp.int32)
    folded = jnp.where(counter < points_all // 2, counter, counter - points_all).astype(jnp.float32)
    lateral = 2.0 * math.pi / points_all * folded
    excess = wave_nums[:, None] ** 2 - lateral[None, :] ** 2
    upward = jnp.sqrt(jnp.maximum(excess, 0.0)) * STEP_DEPTH
    damped = jnp.sqrt(jnp.maximum(-excess, 0.0)) * STEP_DEPTH
    real_part = jnp.where(excess > 0, jnp.cos(upward), jnp.exp(-damped))
    imag_part = jnp.where(excess > 0, jnp.sin(upward), jnp.zeros_like(upward))
    return jnp.stack([real_part, imag_part], axis=1)


def screens(wave_nums, slowness):
    phase = wave_nums[:, None, None] * STEP_DEPTH * slowness[None]
    return jnp.stack([jnp.cos(phase), jnp.sin(phase)], axis=2)


def encoded_sources(incident, encode, sources):
    shifts = jnp.arange(sources, dtype=jnp.int32)
    bit_set = encode[:, None] >> shifts[None, :] & 1
    signs_all = (1 - 2 * bit_set).astype(jnp.float32)
    return jnp.sum(signs_all[:, :, None, None] * incident, axis=1)


def lookup_waves(freq_index, wavenum, table_size):
    onehot_rows = (freq_index[:, None] == jnp.arange(table_size, dtype=jnp.int32)[None, :]).astype(
        jnp.float32
    )
    return jnp.sum(onehot_rows * wavenum[None, :], axis=1)


def shards(incident, encode, freq_index, wavenum, slowness, probes):
    points_all = SIDE * SIDE
    forward = dft_tables(SIDE, -1.0)
    inverse = dft_tables(SIDE, 1.0)
    group_count = incident.shape[0]
    plane_count = slowness.shape[0]
    probe_count = probes.shape[0]
    sources = encoded_sources(incident, encode, incident.shape[1])
    wave_nums = lookup_waves(freq_index, wavenum, wavenum.shape[0])
    spectra = propagator(wave_nums, points_all)
    spectra_back = conjugate(spectra)
    plane_screens = screens(wave_nums, slowness)
    born_scale = wave_nums * STEP_DEPTH
    depth_index = lax.axis_index("depth")
    depth_count = lax.axis_size("depth")

    def march_background(upper):
        current = upper
        current = complex_times(plane_screens[:, 0], propagate(current, spectra, forward, inverse))
        states = [current]
        return states

    source_low = sources.astype(jnp.bfloat16)
    received = jnp.zeros_like(source_low)
    for segment in range(depth_count - 1):
        upper = jnp.where(depth_index == 0, source_low, received)
        passing = march_background(upper)
        received = from_behind(passing[-1].astype(jnp.bfloat16), "depth", 1)
    backgrounds = march_background(jnp.where(depth_index == 0, source_low, received))

    def march_tangent(upper, probe_block):
        current = upper
        moved_on = complex_times(
            plane_screens[:, 0][:, None], propagate(current, spectra[:, None], forward, inverse)
        )
        background = backgrounds[0]
        scaled = born_scale[:, None, None] * probe_block[:, 0].astype(jnp.float32)[None]
        born_term = jnp.stack(
            [-scaled * background[:, None, 1], scaled * background[:, None, 0]], axis=2
        )
        current = moved_on + born_term
        return current

    def march_adjoint(lowest_field):
        adjoint = lowest_field
        pieces = [None] * plane_count
        for plane in reversed(range(plane_count)):
            background = backgrounds[plane]
            product_terms = born_scale[:, None, None] * (
                background[:, None, 0] * adjoint[:, :, 1]
                - background[:, None, 1] * adjoint[:, :, 0]
            )
            pieces[plane] = jnp.sum(product_terms, axis=0)
            turned_back = complex_times(conjugate(plane_screens[:, plane])[:, None], adjoint)
            adjoint = propagate(turned_back, spectra_back[:, None], forward, inverse)
        return (adjoint, jnp.stack(pieces, axis=1))

    block_rows = 4
    block_count = probe_count // block_rows
    segment_count = depth_count + block_count - 1
    field_shape = (group_count, block_rows, 2, points_all)
    received_tangent = jnp.zeros(field_shape, jnp.bfloat16)
    bottoms = jnp.zeros((group_count, probe_count + block_rows, 2, points_all), jnp.float32)
    for segment in range(segment_count):
        position = segment - depth_index
        active = (position >= 0) & (position < block_count)
        chosen = jnp.clip(position, 0, block_count - 1)
        slot = jnp.where(active, chosen * block_rows, probe_count)
        probe_block = lax.dynamic_slice_in_dim(probes, chosen * block_rows, block_rows, 0)
        upper = jnp.where(depth_index == 0, jnp.zeros_like(received_tangent), received_tangent)
        lowest = lax.cond(
            active,
            lambda: march_tangent(upper, probe_block),
            lambda: jnp.zeros(field_shape, jnp.float32),
        )
        bottoms = lax.dynamic_update_slice_in_dim(bottoms, lowest, slot, 1)
        if segment + 1 < segment_count:
            received_tangent = from_behind(lowest.astype(jnp.bfloat16), "depth", 1)
    rank_up = depth_count - 1 - depth_index
    received_adjoint = jnp.zeros(field_shape, jnp.float32)
    sketch_part = jnp.zeros((probe_count + block_rows, plane_count, points_all), jnp.float32)
    for segment in range(segment_count):
        position = segment - rank_up
        active = (position >= 0) & (position < block_count)
        chosen = jnp.clip(position, 0, block_count - 1)
        slot = jnp.where(active, chosen * block_rows, probe_count)
        seeded = lax.dynamic_slice_in_dim(bottoms, chosen * block_rows, block_rows, 1)
        lower_field = jnp.where(depth_index == depth_count - 1, seeded, received_adjoint)
        topmost, block_sketch = lax.cond(
            active,
            lambda: march_adjoint(lower_field),
            lambda: (
                jnp.zeros(field_shape, jnp.float32),
                jnp.zeros((block_rows, plane_count, points_all), jnp.float32),
            ),
        )
        sketch_part = lax.dynamic_update_slice_in_dim(sketch_part, block_sketch, slot, 0)
        if segment + 1 < segment_count:
            received_adjoint = from_behind(topmost.astype(jnp.bfloat16), "depth", -1).astype(
                topmost.dtype
            )
    summed = lax.psum_scatter(sketch_part[:probe_count], "src", scatter_dimension=2, tiled=True)
    src_count = lax.axis_size("src")
    slab_width = summed.shape[2]
    local_probes = lax.dynamic_slice_in_dim(
        probes, lax.axis_index("src") * slab_width, slab_width, 2
    ).astype(jnp.float32)
    sketch = summed / (group_count * src_count) + DAMPING * local_probes
    flattened = sketch.reshape(probe_count, plane_count * slab_width)
    row_total = plane_count * slab_width * src_count * depth_count
    gram_local = jnp.dot(flattened, flattened.T, precision=lax.Precision.HIGHEST) / row_total
    gram_matrix = lax.psum(gram_local, ("src", "depth"))
    lower_factor = jnp.linalg.cholesky(gram_matrix)
    identity = jnp.eye(probe_count, dtype=jnp.float32)
    inverse_lower = lax.linalg.triangular_solve(lower_factor, identity, left_side=True, lower=True)
    sketch_basis = jnp.dot(inverse_lower, flattened, precision=lax.Precision.HIGHEST).reshape(
        probe_count, plane_count, slab_width
    )
    return (sketch_basis, lower_factor.T)


def solution(mesh):
    in_specs = (
        P("src", None, None, None),
        P("src"),
        P("src"),
        P(),
        P("depth", None),
        P(None, "depth", None),
    )
    out_specs = (P(None, "depth", "src"), P())
    return jax.shard_map(shards, mesh=mesh, in_specs=in_specs, out_specs=out_specs, check_vma=False)
```

profile of v0, /device:TPU:1, one launch (start us, length us, event | category | flops | bytes accessed | tf_op | source)
XLA Modules:
  0.0 747.9 jit_solution(17268058572091044971)
XLA Ops:
  38.6 4.6 conditional.38
  47.1 4.5 conditional.39
  56.7 4.5 conditional.40
  66.3 4.5 conditional.41
  76.5 4.5 conditional.42
  86.5 4.5 conditional.43
  96.1 4.5 conditional.44
  105.7 4.5 conditional.45
  115.3 4.5 conditional.46
  124.9 4.5 conditional.47
  134.5 4.5 conditional.48
  144.1 4.5 conditional.49
  153.7 4.5 conditional.50
  163.4 4.5 conditional.51
  173.2 4.4 conditional.52
  183.2 4.4 conditional.53
  193.1 8.1 %collective-permute-start.19 = (bf16[1,4,2,4096]{3,2,1,0:T(2,128)(2,1)S(1)}, bf16[1,4,2,4096]{3,2,1,0:T(2,128)(2,1)S(1)}, u32[]{:S(2)}, u32[]{:S(2)}) collective-permute-start(bf16[1,4,2,4096]{3,2,1,0:T(2,128)(2,1)S(1)} %get-tuple-element.7639), channel_id=1, source_target_pairs={{0,1},{1,2},{2,3},{4,5},{5,6},{6,7},{8,9},{9,10},{10,11},{12,13},{... | collective-permute-start | bytes 196616 | tf_op jit(solution)/shard_map/ppermute | solution.py:15
  209.3 7.0 collective-permute-done.21
  224.6 17.3 %collective-permute-done.23 = bf16[1,4,2,4096]{3,2,1,0:T(2,128)(2,1)S(1)} collective-permute-done((bf16[1,4,2,4096]{3,2,1,0:T(2,128)(2,1)S(1)}, bf16[1,4,2,4096]{3,2,1,0:T(2,128)(2,1)S(1)}, u32[]{:S(2)}, u32[]{:S(2)}) %collective-permute-start.23) | collective-permute-done | bytes 65568 | tf_op jit(solution)/shard_map/ppermute | solution.py:15
  370.0 4.2 conditional.74
  385.8 238.3 %reduce-scatter.4.cloned.1.call-done = f32[32,64]{1,0:T(8,128)} async-done(((f32[4096,64]{1,0:T(8,128)}), f32[32,64]{1,0:T(8,128)}) %reduce-scatter.4.cloned.1.call-update) | async-done | bytes 8208
  626.0 99.9 %psum.7 = f32[64,64]{0,1:T(8,128)S(1)} all-reduce(f32[64,64]{0,1:T(8,128)S(1)} %convolution_multiply_fusion), channel_id=1, replica_groups=mesh['src'=128,'depth'=4] {'src','depth'}, use_global_device_ids=true, to_apply=%region_79.80 | all-reduce | flops 4096 | bytes 32768 | tf_op jit(solution)/shard_map/psum | solution.py:212
  726.0 5.8 cholesky.17
  733.2 4.9 custom-call.6
  (1100 shorter events, 399.2 us)
Async XLA Ops:
  7.2 617.0 %reduce-scatter.4.cloned.1.call-start = ((), (), s32[]{:S(2)}) async-start(), calls=%async_computation.1 | async-start | bytes 2113536
  16.9 5.1 collective-permute-start
  61.3 5.0 collective-permute-start.5
  70.9 5.6 collective-permute-start.6
  81.1 5.3 collective-permute-start.7
  100.7 5.0 collective-permute-start.9
  119.9 5.0 collective-permute-start.11
  139.1 5.0 collective-permute-start.13
  158.3 5.0 collective-permute-start.15
  168.0 5.2 collective-permute-start.16
  177.7 5.5 collective-permute-start.17
  193.1 9.4 %collective-permute-start.19 = (bf16[1,4,2,4096]{3,2,1,0:T(2,128)(2,1)S(1)}, bf16[1,4,2,4096]{3,2,1,0:T(2,128)(2,1)S(1)}, u32[]{:S(2)}, u32[]{:S(2)}) collective-permute-start(bf16[1,4,2,4096]{3,2,1,0:T(2,128)(2,1)S(1)} %get-tuple-element.7639), channel_id=1, source_target_pairs={{0,1},{1,2},{2,3},{4,5},{5,6},{6,7},{8,9},{9,10},{10,11},{12,13},{... | collective-permute-start | bytes 196616 | tf_op jit(solution)/shard_map/ppermute | solution.py:15
  202.6 5.0 collective-permute-start.20
  207.8 8.5 %collective-permute-start.21 = (bf16[1,4,2,4096]{3,2,1,0:T(2,128)(2,1)S(1)}, bf16[1,4,2,4096]{3,2,1,0:T(2,128)(2,1)S(1)}, u32[]{:S(2)}, u32[]{:S(2)}) collective-permute-start(bf16[1,4,2,4096]{3,2,1,0:T(2,128)(2,1)S(1)} %get-tuple-element.4124), channel_id=1, source_target_pairs={{1,0},{2,1},{3,2},{5,4},{6,5},{7,6},{9,8},{10,9},{11,10},{13,12},{... | collective-permute-start | bytes 196616 | tf_op jit(solution)/shard_map/ppermute | solution.py:15
  216.4 5.6 collective-permute-start.22
  222.6 19.2 %collective-permute-start.23 = (bf16[1,4,2,4096]{3,2,1,0:T(2,128)(2,1)S(1)}, bf16[1,4,2,4096]{3,2,1,0:T(2,128)(2,1)S(1)}, u32[]{:S(2)}, u32[]{:S(2)}) collective-permute-start(bf16[1,4,2,4096]{3,2,1,0:T(2,128)(2,1)S(1)} %get-tuple-element.4128), channel_id=1, source_target_pairs={{1,0},{2,1},{3,2},{5,4},{6,5},{7,6},{9,8},{10,9},{11,10},{13,12},{... | collective-permute-start | bytes 196616 | tf_op jit(solution)/shard_map/ppermute | solution.py:15
  245.8 5.0 collective-permute-start.24
  254.8 5.0 collective-permute-start.25
  263.9 5.2 collective-permute-start.26
  273.0 5.3 collective-permute-start.27
  282.4 5.0 collective-permute-start.28
  327.4 5.0 collective-permute-start.33
  336.4 5.5 collective-permute-start.34
  346.0 5.9 collective-permute-start.35
  (18 other events, 92.0 us)
Sparse Core Ops, SparseCore 0:
  386.0 238.1 reduce-scatter.3
where the time goes:
time: 758 us; the launch traced here: 748 us
  waiting for transfers between devices  339 us (45%)
  starting transfers between devices  104 us (14%)
  blocking collectives  99.9 us (13%)
  other arithmetic  82.9 us (11%)
  local copies, waits for them, and re-layouts  66.5 us (9%)
  matrix products  31.1 us (4%)
  between operations  18.6 us (2%)
    unnamed x2, waiting for transfers between devices  238 us
    ppermute x39, starting transfers between devices, from_behind(): return lax.ppermute(x, axis, pairs)  104 us
    ppermute x39, waiting for transfers between devices, from_behind(): return lax.ppermute(x, axis, pairs)  100 us
    psum x1, blocking collectives, shards(): gram_matrix = lax.psum(gram_local, ('src', 'depth'))  99.9 us
    another operation x16, other arithmetic, march_tangent(): jnp.stack([-scaled * background[:, None, 1], scaled * background[:, None,...  25.4 us
  transfers between devices with their start and end apart: 40, of which 39 were waited for; matrix products, arithmetic and copies ran while one was open for 2% of the time, Pallas kernels for 0%

commit v1 on v0

--- a/solution.py
+++ b/solution.py
@@ -209,7 +209,7 @@
     flattened = sketch.reshape(probe_count, plane_count * slab_width)
     row_total = plane_count * slab_width * src_count * depth_count
     gram_local = jnp.dot(flattened, flattened.T, precision=lax.Precision.HIGHEST) / row_total
-    gram_matrix = lax.psum(gram_local, ("src", "depth"))
+    gram_matrix = jnp.sum(lax.all_gather(gram_local, ("src", "depth")), axis=0)
     lower_factor = jnp.linalg.cholesky(gram_matrix)
     identity = jnp.eye(probe_count, dtype=jnp.float32)
     inverse_lower = lax.linalg.triangular_solve(lower_factor, identity, left_side=True, lower=True)

time: 758 us -> 806 us (1.063)
  waiting for transfers between devices: 339 us -> 479 us
  blocking collectives: 99.9 us -> 0 us
    all_gather x0 -> x1, waiting for transfers between devices: none -> 140 us  [shards(): gram_matrix = jnp.sum(lax.all_gather(gram_local, ('src', 'depth')), axis=0)]
    psum x1 -> x0, blocking collectives: 99.9 us -> none  [shards(): gram_matrix = lax.psum(gram_local, ('src', 'depth'))]
    unnamed x2 -> x3, waiting for transfers between devices: 238 us -> 238 us
  transfers between devices with their start and end apart: 40 -> 41, of which waited for: 39 -> 40; matrix products, arithmetic and copies ran while one was open for 2% -> 2% of each run, Pallas kernels for 0% -> 0%
where the time goes in v1:
time: 806 us; the launch traced here: 796 us
  waiting for transfers between devices  479 us (59%)
  starting transfers between devices  104 us (13%)
  other arithmetic  89.7 us (11%)
  local copies, waits for them, and re-layouts  66.5 us (8%)
  matrix products  31.6 us (4%)
  between operations  18.5 us (2%)
    unnamed x3, waiting for transfers between devices  238 us
    all_gather x1, waiting for transfers between devices, shards(): gram_matrix = jnp.sum(lax.all_gather(gram_local, ('src', 'depth')), axis=0)  140 us
    ppermute x39, starting transfers between devices, from_behind(): return lax.ppermute(x, axis, pairs)  104 us
    ppermute x39, waiting for transfers between devices, from_behind(): return lax.ppermute(x, axis, pairs)  100 us
    another operation x16, other arithmetic, march_tangent(): jnp.stack([-scaled * background[:, None, 1], scaled * background[:, None,...  25.4 us
  transfers between devices with their start and end apart: 41, of which 40 were waited for; matrix products, arithmetic and copies ran while one was open for 2% of the time, Pallas kernels for 0%

profile of v1, /device:TPU:1, one launch (start us, length us, event | category | flops | bytes accessed | tf_op | source)
XLA Modules:
  0.0 795.6 jit_solution(4947894359978155703)
XLA Ops:
  38.6 4.6 conditional.38
  47.1 4.5 conditional.39
  56.7 4.5 conditional.40
  66.3 4.5 conditional.41
  76.5 4.5 conditional.42
  86.5 4.5 conditional.43
  96.1 4.5 conditional.44
  105.7 4.5 conditional.45
  115.3 4.5 conditional.46
  124.9 4.5 conditional.47
  134.5 4.5 conditional.48
  144.1 4.5 conditional.49
  153.7 4.5 conditional.50
  163.3 4.5 conditional.51
  173.1 4.4 conditional.52
  183.2 4.4 conditional.53
  193.1 8.1 %collective-permute-start.19 = (bf16[1,4,2,4096]{3,2,1,0:T(2,128)(2,1)S(1)}, bf16[1,4,2,4096]{3,2,1,0:T(2,128)(2,1)S(1)}, u32[]{:S(2)}, u32[]{:S(2)}) collective-permute-start(bf16[1,4,2,4096]{3,2,1,0:T(2,128)(2,1)S(1)} %get-tuple-element.7639), channel_id=1, source_target_pairs={{0,1},{1,2},{2,3},{4,5},{5,6},{6,7},{8,9},{9,10},{10,11},{12,13},{... | collective-permute-start | bytes 196616 | tf_op jit(solution)/shard_map/ppermute | solution.py:15
  209.2 7.1 collective-permute-done.21
  224.5 17.2 %collective-permute-done.23 = bf16[1,4,2,4096]{3,2,1,0:T(2,128)(2,1)S(1)} collective-permute-done((bf16[1,4,2,4096]{3,2,1,0:T(2,128)(2,1)S(1)}, bf16[1,4,2,4096]{3,2,1,0:T(2,128)(2,1)S(1)}, u32[]{:S(2)}, u32[]{:S(2)}) %collective-permute-start.23) | collective-permute-done | bytes 65568 | tf_op jit(solution)/shard_map/ppermute | solution.py:15
  385.8 238.3 %reduce-scatter.4.cloned.1.call-done = f32[32,64]{1,0:T(8,128)} async-done(((f32[4096,64]{1,0:T(8,128)}), f32[32,64]{1,0:T(8,128)}) %reduce-scatter.4.cloned.1.call-update) | async-done | bytes 8208
  626.6 140.0 %all-gather.3.cloned.1.call-done = f32[32768,64]{1,0:T(8,128)} async-done(((f32[64,64]{1,0:T(8,128)}), f32[32768,64]{1,0:T(8,128)}) %all-gather.3.cloned.1.call-update) | async-done | bytes 8388624 | tf_op jit(solution)/shard_map/all_gather | solution.py:212
  766.6 6.9 reduce_sum.38
  773.7 5.8 cholesky.17
  781.6 4.9 custom-call.6
  (1103 shorter events, 403.9 us)
Async XLA Ops:
  7.2 616.9 %reduce-scatter.4.cloned.1.call-start = ((), (), s32[]{:S(2)}) async-start(), calls=%async_computation.2 | async-start | bytes 2113536
  16.9 5.1 collective-permute-start
  51.7 5.0 collective-permute-start.4
  61.3 5.0 collective-permute-start.5
  70.9 5.6 collective-permute-start.6
  81.1 5.4 collective-permute-start.7
  91.1 5.0 collective-permute-start.8
  100.7 5.0 collective-permute-start.9
  110.3 5.0 collective-permute-start.10
  119.9 5.0 collective-permute-start.11
  129.5 5.0 collective-permute-start.12
  167.9 5.2 collective-permute-start.16
  177.7 5.5 collective-permute-start.17
  193.1 9.4 %collective-permute-start.19 = (bf16[1,4,2,4096]{3,2,1,0:T(2,128)(2,1)S(1)}, bf16[1,4,2,4096]{3,2,1,0:T(2,128)(2,1)S(1)}, u32[]{:S(2)}, u32[]{:S(2)}) collective-permute-start(bf16[1,4,2,4096]{3,2,1,0:T(2,128)(2,1)S(1)} %get-tuple-element.7639), channel_id=1, source_target_pairs={{0,1},{1,2},{2,3},{4,5},{5,6},{6,7},{8,9},{9,10},{10,11},{12,13},{... | collective-permute-start | bytes 196616 | tf_op jit(solution)/shard_map/ppermute | solution.py:15
  202.6 5.0 collective-permute-start.20
  207.8 8.5 %collective-permute-start.21 = (bf16[1,4,2,4096]{3,2,1,0:T(2,128)(2,1)S(1)}, bf16[1,4,2,4096]{3,2,1,0:T(2,128)(2,1)S(1)}, u32[]{:S(2)}, u32[]{:S(2)}) collective-permute-start(bf16[1,4,2,4096]{3,2,1,0:T(2,128)(2,1)S(1)} %get-tuple-element.4124), channel_id=1, source_target_pairs={{1,0},{2,1},{3,2},{5,4},{6,5},{7,6},{9,8},{10,9},{11,10},{13,12},{... | collective-permute-start | bytes 196616 | tf_op jit(solution)/shard_map/ppermute | solution.py:15
  216.4 5.6 collective-permute-start.22
  222.6 19.2 %collective-permute-start.23 = (bf16[1,4,2,4096]{3,2,1,0:T(2,128)(2,1)S(1)}, bf16[1,4,2,4096]{3,2,1,0:T(2,128)(2,1)S(1)}, u32[]{:S(2)}, u32[]{:S(2)}) collective-permute-start(bf16[1,4,2,4096]{3,2,1,0:T(2,128)(2,1)S(1)} %get-tuple-element.4128), channel_id=1, source_target_pairs={{1,0},{2,1},{3,2},{5,4},{6,5},{7,6},{9,8},{10,9},{11,10},{13,12},{... | collective-permute-start | bytes 196616 | tf_op jit(solution)/shard_map/ppermute | solution.py:15
  254.8 5.0 collective-permute-start.25
  263.8 5.2 collective-permute-start.26
  273.0 5.4 collective-permute-start.27
  336.3 5.5 collective-permute-start.34
  345.9 5.9 collective-permute-start.35
  385.7 380.9 %all-gather.3.cloned.1.call-start = ((), (), s32[]{:S(2)}) async-start(), calls=%async_computation.1 | async-start | bytes 16809984 | tf_op jit(solution)/shard_map/all_gather | solution.py:212
  (19 other events, 97.0 us)
Sparse Core Ops, SparseCore 0:
  385.8 238.2 reduce-scatter.3
  629.2 137.4 all-gather.2
